TPU v7x, 512 devices: a whole 4x8x8 slice. The times are simulated.
512 devices in a mesh: imp: 32 (over z, x), adv: 16 (over y, core).
Axes of the slice: x: 4, y: 8, z: 8, core: 2. Of those that a mesh axis runs over, the one named last changes fastest.
Arguments:
- impression_vectors: bfloat16 [64, 65536], P(None, 'imp'), may hold values from -6 to 6
- advertiser_vectors: bfloat16 [64, 65536], P(None, ('imp', 'adv')), may hold values from -0.75 to 0.75
- spend_limits: float32 [65536], P(('imp', 'adv')), may hold values from 1024 to 8192
- capacity: float32 [65536], P('imp'), may hold values from 1024 to 8192
- blocks: int32 [512, 16, 8], P('imp', 'adv'), may hold values from 0 to 511, as said below
- counts: int32 [512, 16], P('imp', 'adv'), may hold values from 1 to 8, as said below
Outputs:
- prices: float32 [65536], P(('imp', 'adv'))
- impression_duals: float32 [65536], P('imp')
- impression_grad: bfloat16 [64, 65536], P(None, ('imp', 'adv'))
- advertiser_grad: bfloat16 [64, 65536], P(None, ('imp', 'adv'))
Inputs may be any that keep to these rules, and one draw needn't show every extreme that they name: Block numbers. Entry [g, a, k] names a block b with (b) % (the size of adv) == a. The 8 entries of one list are distinct; entries at slots k >= counts[g, a] are padding and name valid blocks too. `counts`: every group has one index of adv whose count is 8.
All inputs are finite; a program needn't handle non-finite values.
Results may differ from a plain program's by a relative error of at most 0.012.
Values may be sent and summed in bfloat16 or wider, within the bound.
No kernel may reach another device: no remote copies, remote signals or barrier semaphores. Data moves between devices by JAX's collectives and lax.ppermute only.
A program may use at most 64 MiB of HBM per device.

v0:
```python
import jax
import jax.numpy as jnp
from jax import lax
from jax.sharding import PartitionSpec as P

GROUP = 128
BLOCK = 128
ITERS = 3
BLK_DEV = 1


def local(impression_vectors, advertiser_vectors, spend_limits, capacity, blocks, counts):
    features = impression_vectors.shape[0]
    groups_here = blocks.shape[0]
    slot_count = blocks.shape[2]
    adv_devices = lax.axis_size("adv")
    block_ids = blocks.reshape(groups_here, slot_count)
    local_ids = block_ids // BLK_DEV // adv_devices * BLK_DEV + block_ids % BLK_DEV
    live_slots = (jnp.arange(slot_count)[None, :] < counts).astype(jnp.float32)
    viewers = impression_vectors.reshape(features, groups_here, GROUP)
    extent = slot_count * BLOCK
    own_count = spend_limits.shape[0]
    fetched = lax.all_gather(advertiser_vectors, "imp", axis=1, tiled=True)
    catalog = fetched.reshape(features, fetched.shape[1] // BLOCK, BLOCK)
    local_blocks = catalog.shape[1]

    def allocate(source, prices, duals, group_no):
        chosen = lax.dynamic_index_in_dim(local_ids, group_no, 0, keepdims=False)
        columns = jnp.take(source, chosen, axis=1).reshape(features, extent)
        viewer = lax.dynamic_index_in_dim(viewers, group_no, 1, keepdims=False)
        scores = lax.dot_general(
            viewer, columns, (((0,), (0,)), ((), ())), preferred_element_type=jnp.float32
        )
        charged = jnp.take(prices, chosen, axis=0).reshape(extent)
        shadow = lax.dynamic_slice_in_dim(duals, group_no * GROUP, GROUP)
        eligible = jnp.repeat(
            lax.dynamic_index_in_dim(live_slots, group_no, 0, keepdims=False), BLOCK
        )
        shares = jnp.clip(scores - charged[None, :] - shadow[:, None], 0.0, 1.0) * eligible[None, :]
        return (shares, chosen, columns, viewer)

    duals = jnp.zeros((groups_here * GROUP,), jnp.float32)
    range_prices = jnp.zeros((local_blocks, BLOCK), jnp.float32)
    own_prices = jnp.zeros((own_count,), jnp.float32)
    for iteration in range(ITERS):
        totals_prices = range_prices

        def advance(group_no, pair):
            outlay, demand = pair
            shares, chosen, _, _ = allocate(catalog, totals_prices, duals, group_no)
            outlay = outlay.at[chosen].add(jnp.sum(shares, axis=0).reshape(slot_count, BLOCK))
            demand = lax.dynamic_update_slice_in_dim(
                demand, jnp.sum(shares, axis=1), group_no * GROUP, 0
            )
            return (outlay, demand)

        totals_start = (
            jnp.zeros((local_blocks, BLOCK), jnp.float32),
            jnp.zeros((groups_here * GROUP,), jnp.float32),
        )
        outlay, demand = lax.fori_loop(0, groups_here, advance, totals_start)
        own_outlay = lax.psum_scatter(outlay.reshape(-1), "imp", scatter_dimension=0, tiled=True)
        dual_demand = demand
        dual_demand = lax.psum(dual_demand, "adv")
        duals = jnp.maximum(duals + dual_demand / capacity - 1.0, 0.0)
        own_prices = jnp.maximum(own_prices + own_outlay / spend_limits - 1.0, 0.0)
        range_prices = lax.all_gather(own_prices, "imp", axis=0, tiled=True).reshape(
            local_blocks, BLOCK
        )

    def grad_step(group_no, pair):
        imp_part, adv_part = pair
        shares, chosen, columns, viewer = allocate(catalog, range_prices, duals, group_no)
        weights = shares.astype(jnp.bfloat16)
        imp_cols = lax.dot_general(
            columns, weights, (((1,), (1,)), ((), ())), preferred_element_type=jnp.float32
        )
        imp_part = lax.dynamic_update_slice_in_dim(imp_part, imp_cols, group_no * GROUP, 1)
        adv_terms = jnp.dot(viewer, weights, preferred_element_type=jnp.float32).reshape(
            features, slot_count, BLOCK
        )
        adv_part = adv_part.at[:, chosen].add(adv_terms)
        return (imp_part, adv_part)

    start = (
        jnp.zeros((features, groups_here * GROUP), jnp.float32),
        jnp.zeros((features, local_blocks, BLOCK), jnp.float32),
    )
    imp_part, adv_part = lax.fori_loop(0, groups_here, grad_step, start)
    impression_grad = lax.psum_scatter(imp_part, "adv", scatter_dimension=1, tiled=True).astype(
        jnp.bfloat16
    )
    adv_rounded = (adv_part.reshape(features, -1) / GROUP).astype(jnp.bfloat16)
    advertiser_grad = (
        lax.psum_scatter(adv_rounded, "imp", scatter_dimension=1, tiled=True)
        .astype(jnp.float32)
        .astype(jnp.bfloat16)
    )
    return (own_prices, duals, impression_grad, advertiser_grad)


def solution(mesh):
    return jax.shard_map(
        local,
        mesh=mesh,
        in_specs=(
            P(None, "imp"),
            P(None, ("imp", "adv")),
            P(("imp", "adv")),
            P("imp"),
            P("imp", "adv", None),
            P("imp", "adv"),
        ),
        out_specs=(P(("imp", "adv")), P("imp"), P(None, ("imp", "adv")), P(None, ("imp", "adv"))),
        check_vma=False,
    )
```

profile of v0, /device:TPU:25, one launch (start us, length us, event | category | flops | bytes accessed | tf_op | source)
XLA Modules:
  0.0 1180.3 jit_solution(11911110707107156288)
XLA Ops:
  9.5 44.2 %all_gather.12 = bf16[64,4096]{1,0:T(8,128)(2,1)S(1)} all-gather(bf16[64,128]{1,0:T(8,128)(2,1)S(1)} %copy-done.7), channel_id=1, replica_groups=mesh['imp'=32,'adv'=16] {'imp'}, dimensions={1}, use_global_device_ids=true | all-gather | bytes 540672 | tf_op jit(solution)/shard_map/all_gather | solution.py:23
  53.8 41.5 %while.60 = (s32[]{:T(128)}, f32[32,128]{1,0:T(8,128)S(1)}, f32[2048]{0:T(1024)S(1)}, s32[16,8]{1,0:T(8,128)S(1)}, bf16[64,16,128]{2,0,1:T(8,128)(2,1)S(1)}, /*i...) while((s32[]{:T(128)}, f32[32,128]{1,0:T(8,128)S(1)}, ...), condition=%wide.region_4.7_spmd, body=%wide.region_0.6_spmd.sunk | while | flops 17500104 | bytes 485907 | solution.py:61
  95.4 35.8 %psum.21 = f32[2048]{0:T(1024)S(1)} all-reduce(f32[2048]{0:T(1024)S(1)} %get-tuple-element.597), channel_id=1, replica_groups=mesh['imp'=32,'adv'=16] {'adv'}, use_global_device_ids=true, to_apply=%region_6.9 | all-reduce | flops 2048 | bytes 16384 | tf_op jit(solution)/shard_map/psum | solution.py:64
  131.2 112.5 %all-reduce = f32[4096]{0:T(1024)S(1)} all-reduce(f32[4096]{0:T(1024)S(1)} %bitcast.255), channel_id=2, replica_groups=mesh['imp'=32,'adv'=16] {'imp'}, use_global_device_ids=true, to_apply=%region_5.8.clone | all-reduce | flops 4096 | bytes 32768
  243.8 1.3 dynamic-slice
  245.8 28.0 %all-gather = f32[32,1,128]{2,1,0:T(1,128)S(1)} all-gather(f32[1,1,128]{2,1,0:T(1,128)S(1)} %bitcast.260), channel_id=1, replica_groups=mesh['imp'=32,'adv'=16] {'imp'}, dimensions={0}, use_global_device_ids=true | all-gather | bytes 16896 | tf_op jit(solution)/shard_map/all_gather | solution.py:67
  273.8 42.5 %while.61 = (s32[]{:T(128)}, f32[32,128]{1,0:T(8,128)S(1)}, f32[2048]{0:T(1024)S(1)}, s32[16,8]{1,0:T(8,128)S(1)}, bf16[64,16,128]{2,0,1:T(8,128)(2,1)S(1)}, /*i...) while((s32[]{:T(128)}, f32[32,128]{1,0:T(8,128)S(1)}, ...), condition=%wide.region_11.14_spmd, body=%wide.region_7.13_spmd.sunk | while | flops 17631180 | bytes 471067 | solution.py:61
  316.3 58.5 %psum.22 = f32[2048]{0:T(1024)S(1)} all-reduce(f32[2048]{0:T(1024)S(1)} %get-tuple-element.599), channel_id=1, replica_groups=mesh['imp'=32,'adv'=16] {'adv'}, use_global_device_ids=true, to_apply=%region_13.16 | all-reduce | flops 2048 | bytes 16384 | tf_op jit(solution)/shard_map/psum | solution.py:64
  374.8 112.3 %all-reduce.1 = f32[4096]{0:T(1024)S(1)} all-reduce(f32[4096]{0:T(1024)S(1)} %bitcast.256), channel_id=3, replica_groups=mesh['imp'=32,'adv'=16] {'imp'}, use_global_device_ids=true, to_apply=%region_12.15.clone | all-reduce | flops 4096 | bytes 32768
  487.2 27.5 %all-gather.1 = f32[32,1,128]{2,1,0:T(1,128)S(1)} all-gather(f32[1,1,128]{2,1,0:T(1,128)S(1)} %bitcast.259), channel_id=1, replica_groups=mesh['imp'=32,'adv'=16] {'imp'}, dimensions={0}, use_global_device_ids=true | all-gather | bytes 16896 | tf_op jit(solution)/shard_map/all_gather | solution.py:67
  514.7 42.4 %while.62 = (s32[]{:T(128)}, f32[32,128]{1,0:T(8,128)S(1)}, f32[2048]{0:T(1024)S(1)}, s32[16,8]{1,0:T(8,128)S(1)}, bf16[64,16,128]{2,0,1:T(8,128)(2,1)S(1)}, /*i...) while((s32[]{:T(128)}, f32[32,128]{1,0:T(8,128)S(1)}, ...), condition=%wide.region_18.21_spmd, body=%wide.region_14.20_spmd.sunk | while | flops 17631180 | bytes 471067 | solution.py:61
  557.1 59.3 %psum.23 = f32[2048]{0:T(1024)S(1)} all-reduce(f32[2048]{0:T(1024)S(1)} %get-tuple-element.601), channel_id=1, replica_groups=mesh['imp'=32,'adv'=16] {'adv'}, use_global_device_ids=true, to_apply=%region_20.23 | all-reduce | flops 2048 | bytes 16384 | tf_op jit(solution)/shard_map/psum | solution.py:64
  617.1 111.9 %all-reduce.2 = f32[4096]{0:T(1024)S(1)} all-reduce(f32[4096]{0:T(1024)S(1)} %bitcast.257), channel_id=4, replica_groups=mesh['imp'=32,'adv'=16] {'imp'}, use_global_device_ids=true, to_apply=%region_19.22.clone | all-reduce | flops 4096 | bytes 32768
  729.6 27.5 %all-gather.2 = f32[32,1,128]{2,1,0:T(1,128)S(1)} all-gather(f32[1,1,128]{2,1,0:T(1,128)S(1)} %bitcast.261), channel_id=1, replica_groups=mesh['imp'=32,'adv'=16] {'imp'}, dimensions={0}, use_global_device_ids=true | all-gather | bytes 16896 | tf_op jit(solution)/shard_map/all_gather | solution.py:67
  757.2 95.1 %while.63 = (s32[]{:T(128)}, f32[64,2048]{1,0:T(8,128)S(1)}, f32[64,32,128]{2,0,1:T(8,128)S(1)}, s32[16,8]{1,0:T(8,128)S(1)}, bf16[64,32,128]{2,0,1:T(8,128)(2,1...) while((s32[]{:T(128)}, f32[64,2048]{1,0:T(8,128)S(1)}, ...), condition=%wide.region_23.26_spmd, body=%wide.region_21.25_spmd.sunk | while | flops 51185740 | bytes 2993603 | solution.py:89
  757.8 0.8 dynamic_slice.201
  762.2 0.9 scatter_fusion
  763.7 0.8 dynamic_slice.201
  768.2 0.9 scatter_fusion
  769.7 0.8 dynamic_slice.201
  774.1 0.9 scatter_fusion
  775.6 0.8 dynamic_slice.201
  780.0 0.9 scatter_fusion
  781.6 0.8 dynamic_slice.201
  786.0 0.9 scatter_fusion
  787.5 0.8 dynamic_slice.201
  791.9 0.9 scatter_fusion
  793.5 0.8 dynamic_slice.201
  797.9 0.9 scatter_fusion
  799.4 0.8 dynamic_slice.201
  803.8 0.9 scatter_fusion
  805.4 0.8 dynamic_slice.201
  809.8 0.9 scatter_fusion
  811.3 0.8 dynamic_slice.201
  815.7 0.9 scatter_fusion
  821.7 0.9 scatter_fusion
  823.2 0.8 dynamic_slice.201
  827.6 0.9 scatter_fusion
  833.6 0.9 scatter_fusion
  839.5 0.9 scatter_fusion
  841.0 0.8 dynamic_slice.201
  845.4 0.9 scatter_fusion
  851.4 0.9 scatter_fusion
  853.1 1.3 copy.68
  855.3 250.8 %reduce-scatter.7.cloned.1.call-done = bf16[128,64]{1,0:T(8,128)(2,1)} async-done(((bf16[4096,64]{1,0:T(8,128)(2,1)}), bf16[128,64]{1,0:T(8,128)(2,1)}) %reduce-scatter.7.cloned.1.call-update) | async-done | bytes 16400
  1106.1 1.4 copy.67
  1107.5 64.6 %reduce-scatter.5.cloned.1.call-done = f32[64,128]{1,0:T(8,128)} async-done(((f32[64,2048]{1,0:T(8,128)}), f32[64,128]{1,0:T(8,128)}) %reduce-scatter.5.cloned.1.call-update) | async-done | bytes 32784 | tf_op jit(solution)/shard_map/reduce_scatter | solution.py:90
  1172.1 1.4 convert_element_type.23
  (972 shorter events, 198.5 us)
Async XLA Ops:
  7.2 1.6 copy-start
  7.2 1098.9 %reduce-scatter.7.cloned.1.call-start = ((), (), s32[]{:S(2)}) async-start(), calls=%async_computation.3 | async-start | bytes 1081344
  245.8 28.0 %copy-start.2 = (f32[2048]{0:T(1024)S(1)}, f32[2048]{0:T(1024)}, u32[]{:S(2)}) copy-start(f32[2048]{0:T(1024)} %param.21) | copy-start | bytes 24580
  757.2 2.0 copy-start.5
  759.2 1.2 copy-start.3
  762.2 0.9 copy-start.10
  763.1 2.0 copy-start.5
  765.1 1.2 copy-start.3
  768.2 0.9 copy-start.10
  769.1 2.0 copy-start.5
  771.1 1.2 copy-start.3
  774.1 0.9 copy-start.10
  775.0 2.0 copy-start.5
  777.0 1.2 copy-start.3
  780.0 0.9 copy-start.10
  781.0 2.0 copy-start.5
  783.0 1.2 copy-start.3
  786.0 0.9 copy-start.10
  786.9 2.0 copy-start.5
  788.9 1.2 copy-start.3
  791.9 0.9 copy-start.10
  792.9 2.0 copy-start.5
  794.8 1.2 copy-start.3
  797.9 0.9 copy-start.10
  798.8 2.0 copy-start.5
  800.8 1.2 copy-start.3
  803.8 0.9 copy-start.10
  804.8 2.0 copy-start.5
  806.7 1.2 copy-start.3
  809.8 0.9 copy-start.10
  810.7 2.0 copy-start.5
  812.7 1.2 copy-start.3
  815.7 0.9 copy-start.10
  816.7 2.0 copy-start.5
  818.6 1.2 copy-start.3
  821.7 0.9 copy-start.10
  822.6 2.0 copy-start.5
  824.6 1.2 copy-start.3
  827.6 0.9 copy-start.10
  828.5 2.0 copy-start.5
  830.5 1.2 copy-start.3
  834.5 2.0 copy-start.5
  836.5 1.2 copy-start.3
  840.4 2.0 copy-start.5
  842.4 1.2 copy-start.3
  846.4 2.0 copy-start.5
  848.4 1.2 copy-start.3
  854.5 317.6 %reduce-scatter.5.cloned.1.call-start = ((), (), s32[]{:S(2)}) async-start(), calls=%async_computation.2 | async-start | bytes 557056 | tf_op jit(solution)/shard_map/reduce_scatter | solution.py:90
  (74 other events, 52.7 us)
Sparse Core Ops, SparseCore 0:
  854.6 251.3 reduce-scatter.6
  1108.8 63.2 reduce-scatter.4
where the time goes:
time: 1180 us
  blocking collectives  617 us (52%)
  waiting for transfers between devices  316 us (27%)
  local copies, waits for them, and re-layouts  133 us (11%)
  other arithmetic  62.3 us (5%)
  matrix products  30.7 us (3%)
  between operations  14.9 us (1%)
    unnamed x3, blocking collectives  337 us
    unnamed x3, waiting for transfers between devices  252 us
    psum x3, blocking collectives, local(): dual_demand = lax.psum(dual_demand, 'adv')  154 us
    all_gather x3, blocking collectives, local(): lax.all_gather(own_prices, 'imp', axis=0, tiled=True)  83 us
    reduce_scatter x1, waiting for transfers between devices, local(): lax.psum_scatter(imp_part, 'adv', scatter_dimension=1, tiled=True)  64.6 us
    all_gather x1, blocking collectives, local(): fetched = lax.all_gather(advertiser_vectors, 'imp', axis=1, tiled=True)  44.2 us
    gather x64, local copies, waits for them, and re-layouts, allocate(): columns = jnp.take(source, chosen, axis=1).reshape(features, extent)  36.6 us
    gather x64, local copies, waits for them, and re-layouts, allocate(): charged = jnp.take(prices, chosen, axis=0).reshape(extent)  35.6 us
  transfers between devices with their start and end apart: 2, of which 2 were waited for; matrix products, arithmetic and copies ran while one was open for 0% of the time, Pallas kernels for 0%

commit v1 on v0

--- a/solution.py
+++ b/solution.py
@@ -61,7 +61,7 @@
         outlay, demand = lax.fori_loop(0, groups_here, advance, totals_start)
         own_outlay = lax.psum_scatter(outlay.reshape(-1), "imp", scatter_dimension=0, tiled=True)
         dual_demand = demand
-        dual_demand = lax.psum(dual_demand, "adv")
+        dual_demand = jnp.sum(lax.all_gather(dual_demand, "adv"), axis=0)
         duals = jnp.maximum(duals + dual_demand / capacity - 1.0, 0.0)
         own_prices = jnp.maximum(own_prices + own_outlay / spend_limits - 1.0, 0.0)
         range_prices = lax.all_gather(own_prices, "imp", axis=0, tiled=True).reshape(

time: 1180 us -> 1160 us (0.983)
  the two profiles are of different devices: /device:TPU:25 before, /device:TPU:2 now
where the time goes in v1:
time: 1160 us; the launch traced here: 1150 us
  blocking collectives  630 us (54%)
  waiting for transfers between devices  277 us (24%)
  local copies, waits for them, and re-layouts  134 us (12%)
  other arithmetic  62.4 us (5%)
  matrix products  30.7 us (3%)
  between operations  14.9 us (1%)
    unnamed x3, blocking collectives  404 us
    unnamed x3, waiting for transfers between devices  218 us
    all_gather x3, blocking collectives, local(): lax.all_gather(own_prices, 'imp', axis=0, tiled=True)  121 us
    reduce_scatter x1, waiting for transfers between devices, local(): lax.psum_scatter(imp_part, 'adv', scatter_dimension=1, tiled=True)  59.5 us
    all_gather x1, blocking collectives, local(): fetched = lax.all_gather(advertiser_vectors, 'imp', axis=1, tiled=True)  56.1 us
    all_gather x3, blocking collectives, local(): dual_demand = jnp.sum(lax.all_gather(dual_demand, 'adv'), axis=0)  48.8 us
    gather x64, local copies, waits for them, and re-layouts, allocate(): columns = jnp.take(source, chosen, axis=1).reshape(features, extent)  36.6 us
    gather x64, local copies, waits for them, and re-layouts, allocate(): charged = jnp.take(prices, chosen, axis=0).reshape(extent)  35.6 us
  transfers between devices with their start and end apart: 2, of which 2 were waited for; matrix products, arithmetic and copies ran while one was open for 0% of the time, Pallas kernels for 0%

profile of v1, /device:TPU:2, one launch (start us, length us, event | category | flops | bytes accessed | tf_op | source)
XLA Modules:
  0.0 1154.9 jit_solution(15267386383275936828)
XLA Ops:
  9.5 56.1 %all_gather.30 = bf16[64,4096]{1,0:T(8,128)(2,1)S(1)} all-gather(bf16[64,128]{1,0:T(8,128)(2,1)S(1)} %copy-done.7), channel_id=1, replica_groups=mesh['imp'=32,'adv'=16] {'imp'}, dimensions={1}, use_global_device_ids=true | all-gather | bytes 540672 | tf_op jit(solution)/shard_map/all_gather | solution.py:23
  65.8 41.5 %while.60 = (s32[]{:T(128)}, f32[32,128]{1,0:T(8,128)S(1)}, f32[2048]{0:T(1024)S(1)}, s32[16,8]{1,0:T(8,128)S(1)}, bf16[64,16,128]{2,0,1:T(8,128)(2,1)S(1)}, /*i...) while((s32[]{:T(128)}, f32[32,128]{1,0:T(8,128)S(1)}, ...), condition=%wide.region_4.7_spmd, body=%wide.region_0.6_spmd.sunk | while | flops 17500104 | bytes 485907 | solution.py:61
  107.3 135.6 %all-reduce = f32[4096]{0:T(1024)S(1)} all-reduce(f32[4096]{0:T(1024)S(1)} %bitcast.255), channel_id=5, replica_groups=mesh['imp'=32,'adv'=16] {'imp'}, use_global_device_ids=true, to_apply=%region_5.8.clone | all-reduce | flops 4096 | bytes 32768
  242.9 1.3 dynamic-slice
  244.9 40.1 %all-gather.3 = f32[32,1,128]{2,1,0:T(1,128)S(1)} all-gather(f32[1,1,128]{2,1,0:T(1,128)S(1)} %bitcast.260), channel_id=1, replica_groups=mesh['imp'=32,'adv'=16] {'imp'}, dimensions={0}, use_global_device_ids=true | all-gather | bytes 16896 | tf_op jit(solution)/shard_map/all_gather | solution.py:67
  285.0 17.9 %all-gather = f32[32768]{0:T(1024)S(1)} all-gather(f32[2048]{0:T(1024)S(1)} %get-tuple-element.597), channel_id=2, replica_groups=mesh['imp'=32,'adv'=16] {'adv'}, dimensions={0}, use_global_device_ids=true | all-gather | bytes 139264 | tf_op jit(solution)/shard_map/all_gather | solution.py:64
  303.7 42.5 %while.61 = (s32[]{:T(128)}, f32[32,128]{1,0:T(8,128)S(1)}, f32[2048]{0:T(1024)S(1)}, s32[16,8]{1,0:T(8,128)S(1)}, bf16[64,16,128]{2,0,1:T(8,128)(2,1)S(1)}, /*i...) while((s32[]{:T(128)}, f32[32,128]{1,0:T(8,128)S(1)}, ...), condition=%wide.region_11.14_spmd, body=%wide.region_7.13_spmd.sunk | while | flops 17631180 | bytes 471067 | solution.py:61
  346.2 134.6 %all-reduce.1 = f32[4096]{0:T(1024)S(1)} all-reduce(f32[4096]{0:T(1024)S(1)} %bitcast.256), channel_id=6, replica_groups=mesh['imp'=32,'adv'=16] {'imp'}, use_global_device_ids=true, to_apply=%region_12.15.clone | all-reduce | flops 4096 | bytes 32768
  480.8 40.4 %all-gather.4 = f32[32,1,128]{2,1,0:T(1,128)S(1)} all-gather(f32[1,1,128]{2,1,0:T(1,128)S(1)} %bitcast.259), channel_id=1, replica_groups=mesh['imp'=32,'adv'=16] {'imp'}, dimensions={0}, use_global_device_ids=true | all-gather | bytes 16896 | tf_op jit(solution)/shard_map/all_gather | solution.py:67
  521.2 15.3 %all-gather.1 = f32[32768]{0:T(1024)S(1)} all-gather(f32[2048]{0:T(1024)S(1)} %get-tuple-element.599), channel_id=3, replica_groups=mesh['imp'=32,'adv'=16] {'adv'}, dimensions={0}, use_global_device_ids=true | all-gather | bytes 139264 | tf_op jit(solution)/shard_map/all_gather | solution.py:64
  536.6 42.5 %while.62 = (s32[]{:T(128)}, f32[32,128]{1,0:T(8,128)S(1)}, f32[2048]{0:T(1024)S(1)}, s32[16,8]{1,0:T(8,128)S(1)}, bf16[64,16,128]{2,0,1:T(8,128)(2,1)S(1)}, /*i...) while((s32[]{:T(128)}, f32[32,128]{1,0:T(8,128)S(1)}, ...), condition=%wide.region_18.21_spmd, body=%wide.region_14.20_spmd.sunk | while | flops 17631180 | bytes 471067 | solution.py:61
  579.1 134.4 %all-reduce.2 = f32[4096]{0:T(1024)S(1)} all-reduce(f32[4096]{0:T(1024)S(1)} %bitcast.257), channel_id=7, replica_groups=mesh['imp'=32,'adv'=16] {'imp'}, use_global_device_ids=true, to_apply=%region_19.22.clone | all-reduce | flops 4096 | bytes 32768
  714.0 40.2 %all-gather.5 = f32[32,1,128]{2,1,0:T(1,128)S(1)} all-gather(f32[1,1,128]{2,1,0:T(1,128)S(1)} %bitcast.261), channel_id=1, replica_groups=mesh['imp'=32,'adv'=16] {'imp'}, dimensions={0}, use_global_device_ids=true | all-gather | bytes 16896 | tf_op jit(solution)/shard_map/all_gather | solution.py:67
  754.3 15.7 %all-gather.2 = f32[32768]{0:T(1024)S(1)} all-gather(f32[2048]{0:T(1024)S(1)} %get-tuple-element.601), channel_id=4, replica_groups=mesh['imp'=32,'adv'=16] {'adv'}, dimensions={0}, use_global_device_ids=true | all-gather | bytes 139264 | tf_op jit(solution)/shard_map/all_gather | solution.py:64
  770.8 95.1 %while.63 = (s32[]{:T(128)}, f32[64,2048]{1,0:T(8,128)S(1)}, f32[64,32,128]{2,0,1:T(8,128)S(1)}, s32[16,8]{1,0:T(8,128)S(1)}, bf16[64,32,128]{2,0,1:T(8,128)(2,1...) while((s32[]{:T(128)}, f32[64,2048]{1,0:T(8,128)S(1)}, ...), condition=%wide.region_23.26_spmd, body=%wide.region_21.25_spmd.sunk | while | flops 51185740 | bytes 2993603 | solution.py:89
  771.4 0.8 dynamic_slice.201
  775.8 0.9 scatter_fusion
  777.3 0.8 dynamic_slice.201
  781.7 0.9 scatter_fusion
  783.3 0.8 dynamic_slice.201
  787.7 0.9 scatter_fusion
  789.2 0.8 dynamic_slice.201
  793.6 0.9 scatter_fusion
  795.2 0.8 dynamic_slice.201
  799.6 0.9 scatter_fusion
  801.1 0.8 dynamic_slice.201
  805.5 0.9 scatter_fusion
  807.1 0.8 dynamic_slice.201
  811.5 0.9 scatter_fusion
  813.0 0.8 dynamic_slice.201
  817.4 0.9 scatter_fusion
  818.9 0.8 dynamic_slice.201
  823.4 0.9 scatter_fusion
  824.9 0.8 dynamic_slice.201
  829.3 0.9 scatter_fusion
  835.2 0.9 scatter_fusion
  841.2 0.9 scatter_fusion
  847.1 0.9 scatter_fusion
  853.1 0.9 scatter_fusion
  854.6 0.8 dynamic_slice.201
  859.0 0.9 scatter_fusion
  860.6 0.8 dynamic_slice.201
  865.0 0.9 scatter_fusion
  866.7 1.3 copy.86
  868.8 216.9 %reduce-scatter.7.cloned.1.call-done = bf16[128,64]{1,0:T(8,128)(2,1)} async-done(((bf16[4096,64]{1,0:T(8,128)(2,1)}), bf16[128,64]{1,0:T(8,128)(2,1)}) %reduce-scatter.7.cloned.1.call-update) | async-done | bytes 16400
  1085.7 1.4 copy.85
  1087.2 59.5 %reduce-scatter.5.cloned.1.call-done = f32[64,128]{1,0:T(8,128)} async-done(((f32[64,2048]{1,0:T(8,128)}), f32[64,128]{1,0:T(8,128)}) %reduce-scatter.5.cloned.1.call-update) | async-done | bytes 32784 | tf_op jit(solution)/shard_map/reduce_scatter | solution.py:90
  1146.7 1.4 convert_element_type.23
  (978 shorter events, 199.4 us)
Async XLA Ops:
  7.2 1.6 copy-start
  7.2 1078.5 %reduce-scatter.7.cloned.1.call-start = ((), (), s32[]{:S(2)}) async-start(), calls=%async_computation.3 | async-start | bytes 1081344
  770.8 2.0 copy-start.5
  772.8 1.2 copy-start.3
  775.8 0.9 copy-start.10
  776.7 2.0 copy-start.5
  778.7 1.2 copy-start.3
  781.7 0.9 copy-start.10
  782.7 2.0 copy-start.5
  784.6 1.2 copy-start.3
  787.7 0.9 copy-start.10
  788.6 2.0 copy-start.5
  790.6 1.2 copy-start.3
  793.6 0.9 copy-start.10
  794.6 2.0 copy-start.5
  796.5 1.2 copy-start.3
  799.6 0.9 copy-start.10
  800.5 2.0 copy-start.5
  802.5 1.2 copy-start.3
  805.5 0.9 copy-start.10
  806.5 2.0 copy-start.5
  808.4 1.2 copy-start.3
  811.5 0.9 copy-start.10
  812.4 2.0 copy-start.5
  814.4 1.2 copy-start.3
  817.4 0.9 copy-start.10
  818.4 2.0 copy-start.5
  820.3 1.2 copy-start.3
  823.4 0.9 copy-start.10
  824.3 2.0 copy-start.5
  826.3 1.2 copy-start.3
  829.3 0.9 copy-start.10
  830.2 2.0 copy-start.5
  832.2 1.2 copy-start.3
  835.2 0.9 copy-start.10
  836.2 2.0 copy-start.5
  838.2 1.2 copy-start.3
  841.2 0.9 copy-start.10
  842.1 2.0 copy-start.5
  844.1 1.2 copy-start.3
  847.1 0.9 copy-start.10
  848.1 2.0 copy-start.5
  850.0 1.2 copy-start.3
  854.0 2.0 copy-start.5
  856.0 1.2 copy-start.3
  860.0 2.0 copy-start.5
  861.9 1.2 copy-start.3
  868.1 278.6 %reduce-scatter.5.cloned.1.call-start = ((), (), s32[]{:S(2)}) async-start(), calls=%async_computation.2 | async-start | bytes 557056 | tf_op jit(solution)/shard_map/reduce_scatter | solution.py:90
  (74 other events, 52.5 us)
Sparse Core Ops, SparseCore 0:
  868.2 217.4 reduce-scatter.6
  1088.5 58.1 reduce-scatter.4
